TPU v7x, 32 devices: a whole 2x2x4 slice. The times are simulated.
32 devices in a mesh: expert: 8 (over y, x, core), tensor: 4 (over z).
Axes of the slice: x: 2, y: 2, z: 4, core: 2. Of those that a mesh axis runs over, the one named last changes fastest.
Arguments:
- inputs: float32 [7880, 512], P('expert'), may hold values from -6 to 6
- cotangent: float32 [7880, 512], P('expert'), may hold values from -6 to 6
- routes: int32 [2, 7880, 2], P(None, 'expert'), may hold values from 0 to 7, all different within a row
- priority: int32 [2, 7880], P(None, 'expert'), may hold values from 0 to 984, as said below
- attend_in: float32 [2, 3, 512, 512], P(None, None, 'expert', 'tensor'), may hold values from -0.375 to 0.375
- attend_out: float32 [2, 512, 512], P(None, 'tensor', 'expert'), may hold values from -1.5 to 1.5
- router: float32 [2, 512, 8], P(None, None, 'expert'), may hold values from -0.1875 to 0.1875
- norm_gains: float32 [2, 2, 512], P(None, None, 'expert'), may hold values from 0.25 to 1.75
- expert_in: float32 [2, 8, 512, 2048], P(None, 'expert', None, 'tensor'), may hold values from -0.25 to 0.25
- expert_out: float32 [2, 8, 2048, 512], P(None, 'expert', 'tensor'), may hold values from -0.5 to 0.5
Outputs:
- outputs: float32 [7880, 512], P('expert')
- input_grad: float32 [7880, 512], P('expert')
- attend_in_grad: float32 [2, 3, 512, 512], P(None, None, 'expert', 'tensor')
- attend_out_grad: float32 [2, 512, 512], P(None, 'tensor', 'expert')
- router_grad: float32 [2, 512, 8], P(None, None, 'expert')
- gains_grad: float32 [2, 2, 512], P(None, None, 'expert')
- expert_in_grad: float32 [2, 8, 512, 2048], P(None, 'expert', None, 'tensor')
- expert_out_grad: float32 [2, 8, 2048, 512], P(None, 'expert', 'tensor')
Inputs may be any that keep to these rules, and one draw needn't show every extreme that they name: `routes`: in each block each token names two different experts, and every expert is named by some token. `priority`: in each block, the values within each device's 985 tokens are a permutation.
All inputs are finite; a program needn't handle non-finite values.
Results may differ from a plain program's by a relative error of at most 0.025.
The roundings to bfloat16 on the way count: a program that leaves them out, or rounds other values in their place, can miss the bound.
Values may be sent and summed in bfloat16 or wider, within the bound.
A program may use at most 192 MiB of HBM per device.

v0:
```python
import jax
import jax.numpy as jnp
from jax import lax
from jax.sharding import PartitionSpec as P

HEAD_DIM = 64
SEQ = 197


def norm_rows(rows_in, gain_row):
    centred = rows_in - jnp.mean(rows_in, axis=-1, keepdims=True)
    spread = jnp.mean(centred * centred, axis=-1, keepdims=True)
    return centred * lax.rsqrt(spread + 1e-06) * gain_row


def gelu_exact(rows_in):
    return 0.5 * rows_in * (1.0 + lax.erf(rows_in * 0.7071067811865476))


def contract_rows(left_side, right_side):
    return lax.dot_general(
        left_side, right_side, (((0,), (0,)), ((), ())), preferred_element_type=jnp.float32
    )


def contract_last(left_side, right_side):
    return lax.dot_general(
        left_side, right_side, (((1,), (1,)), ((), ())), preferred_element_type=jnp.float32
    )


def heads_total(partial_sum):
    return lax.psum(partial_sum, "tensor")


def to_experts(make_rows, model_width):
    return lax.all_to_all(
        make_rows(0, model_width), "expert", split_axis=0, concat_axis=0, tiled=True
    )


def to_sources(partial_rows):
    shares = lax.psum_scatter(partial_rows, "tensor", scatter_dimension=2, tiled=True)
    moved = lax.all_to_all(
        shares.astype(jnp.bfloat16), "expert", split_axis=0, concat_axis=0, tiled=True
    )
    return lax.all_gather(moved, "tensor", axis=2, tiled=True)


def slot_plan(chosen, rank_rows, experts, capacity):
    columns = lax.broadcasted_iota(jnp.int32, (1, experts), 1)
    first_hot = (chosen[:, 0:1] == columns).astype(jnp.bfloat16)
    second = (chosen[:, 1:2] == columns).astype(jnp.bfloat16)
    earlier = (rank_rows[None, :] < rank_rows[:, None]).astype(jnp.bfloat16)
    count_first = jnp.dot(earlier, first_hot, preferred_element_type=jnp.float32)
    count_second = jnp.dot(earlier, second, preferred_element_type=jnp.float32)
    first_f = first_hot.astype(jnp.float32)
    second_f = second.astype(jnp.float32)
    filled = jnp.sum(first_f, axis=0, keepdims=True)
    slot_first = jnp.sum(count_first * first_f, axis=1)
    slot_second = jnp.sum((filled + count_second) * second_f, axis=1)
    slot_nums = jnp.stack([slot_first, slot_second], axis=1).astype(jnp.int32)
    target = jnp.where(slot_nums < capacity, chosen * capacity + slot_nums, experts * capacity)
    return (target, first_f, second_f)


def local(
    inputs,
    cotangent,
    routes,
    priority,
    attend_in,
    attend_out,
    router,
    norm_gains,
    expert_in,
    expert_out,
):
    experts = lax.axis_size("expert")
    tokens = inputs.shape[0]
    model_width = inputs.shape[1]
    images = tokens // SEQ
    local_heads = attend_in.shape[3] // HEAD_DIM
    layers = attend_in.shape[0]
    capacity = max(2, (10 * tokens + 4 * experts - 1) // (4 * experts))
    slots_all = experts * capacity
    score_scale = HEAD_DIM ** (-0.5)
    in_full, out_full, router_full, gains_full = (
        lax.all_gather(attend_in.astype(jnp.bfloat16), "expert", axis=2, tiled=True),
        lax.all_gather(attend_out.astype(jnp.bfloat16), "expert", axis=2, tiled=True),
        lax.all_gather(router.astype(jnp.bfloat16), "expert", axis=2, tiled=True),
        lax.all_gather(norm_gains.astype(jnp.bfloat16), "expert", axis=2, tiled=True),
    )
    slot_ids = lax.broadcasted_iota(jnp.int32, (1, slots_all), 1)
    stream = inputs
    stash_list = []
    for layer_index in range(layers):
        gains_now = gains_full[layer_index].astype(jnp.float32)
        normed = norm_rows(stream, gains_now[0]).astype(jnp.bfloat16)
        project = in_full[layer_index]
        triple = jnp.einsum(
            "td,jdh->jth", normed, project, preferred_element_type=jnp.float32
        ).astype(jnp.bfloat16)
        shaped = triple.reshape(3, images, SEQ, local_heads, HEAD_DIM)
        scores = (
            jnp.einsum("iqhd,ikhd->ihqk", shaped[0], shaped[1], preferred_element_type=jnp.float32)
            * score_scale
        )
        log_total = jax.nn.logsumexp(scores, axis=-1, keepdims=True)
        attention = jnp.exp(scores - log_total).astype(jnp.bfloat16)
        mixed_heads = (
            jnp.einsum("ihqk,ikhd->iqhd", attention, shaped[2], preferred_element_type=jnp.float32)
            .astype(jnp.bfloat16)
            .reshape(tokens, -1)
        )
        middle = stream + heads_total(
            jnp.dot(mixed_heads, out_full[layer_index], preferred_element_type=jnp.float32)
        )
        normed_two = norm_rows(middle, gains_now[1]).astype(jnp.bfloat16)
        logits = jnp.dot(normed_two, router_full[layer_index], preferred_element_type=jnp.float32)
        probs_all = jax.nn.softmax(logits, axis=-1)
        chosen = routes[layer_index]
        gate_values = jnp.take_along_axis(probs_all, chosen, axis=1)
        target, first_f, second_f = slot_plan(chosen, priority[layer_index], experts, capacity)
        pick_first = (target[:, 0:1] == slot_ids).astype(jnp.bfloat16)
        pick_second = (target[:, 1:2] == slot_ids).astype(jnp.bfloat16)
        pick_both = pick_first + pick_second

        def dispatch_rows(first_col, col_count, normed_two=normed_two, pick_both=pick_both):
            return (
                contract_rows(pick_both, normed_two)
                .astype(jnp.bfloat16)
                .reshape(experts, capacity, col_count)
            )

        arrived = to_experts(dispatch_rows, model_width).reshape(slots_all, model_width)
        win_now = expert_in[layer_index, 0].astype(jnp.bfloat16)
        wout_now = expert_out[layer_index, 0].astype(jnp.bfloat16)
        before = jnp.dot(arrived, win_now, preferred_element_type=jnp.float32)
        hidden = gelu_exact(before).astype(jnp.bfloat16)
        expert_rows = jnp.dot(hidden, wout_now, preferred_element_type=jnp.float32).reshape(
            experts, capacity, model_width
        )
        returned = to_sources(expert_rows).reshape(slots_all, model_width)
        rows_first = jnp.dot(pick_first, returned, preferred_element_type=jnp.float32)
        rows_second = jnp.dot(pick_second, returned, preferred_element_type=jnp.float32)
        output = middle + gate_values[:, 0:1] * rows_first + gate_values[:, 1:2] * rows_second
        kept_pre = None
        stash_list.append(
            (
                stream,
                gains_now,
                normed,
                shaped,
                log_total,
                mixed_heads,
                middle,
                normed_two,
                probs_all,
                gate_values,
                target,
                first_f,
                second_f,
                pick_first,
                pick_second,
                pick_both,
                arrived,
                rows_first,
                rows_second,
                kept_pre,
            )
        )
        stream = output
    upstream = cotangent
    grads_in, grads_out, grads_router, grads_gain, grads_win, grads_wout = ([], [], [], [], [], [])
    for layer_index in reversed(range(layers)):
        (
            stream_in,
            gains_now,
            normed,
            shaped,
            log_total,
            mixed_heads,
            middle,
            normed_two,
            probs_all,
            gate_values,
            target,
            first_f,
            second_f,
            pick_first,
            pick_second,
            pick_both,
            arrived,
            rows_first,
            rows_second,
            kept_pre,
        ) = stash_list[layer_index]
        win_now = expert_in[layer_index, 0].astype(jnp.bfloat16)
        wout_now = expert_out[layer_index, 0].astype(jnp.bfloat16)
        gate_first = jnp.sum(upstream * rows_first, axis=1)
        gate_second = jnp.sum(upstream * rows_second, axis=1)
        scaled = jnp.concatenate(
            [
                gate_values[:, 0:1] * upstream,
                gate_values[:, 1:2] * upstream,
                jnp.zeros((1, model_width), jnp.float32),
            ],
            axis=0,
        )
        owners = (
            jnp.full((slots_all + 1,), 2 * tokens, jnp.int32)
            .at[jnp.concatenate([target[:, 0], target[:, 1]])]
            .set(jnp.arange(2 * tokens, dtype=jnp.int32))[:slots_all]
        )

        def gradient_rows(first_col, col_count, scaled=scaled, owners=owners):
            return (
                jnp.take(scaled, owners, axis=0)
                .astype(jnp.bfloat16)
                .reshape(experts, capacity, col_count)
            )

        grad_arrived = to_experts(gradient_rows, model_width).reshape(slots_all, model_width)
        before = jnp.dot(arrived, win_now, preferred_element_type=jnp.float32)
        hidden = gelu_exact(before).astype(jnp.bfloat16)
        grads_wout.append(contract_rows(hidden, grad_arrived))
        grad_hidden = contract_last(grad_arrived, wout_now)
        grad_before = jax.vjp(gelu_exact, before)[1](grad_hidden)[0].astype(jnp.bfloat16)
        grads_win.append(contract_rows(arrived, grad_before))
        grad_rows = contract_last(grad_before, win_now).reshape(experts, capacity, model_width)
        grad_dispatched = to_sources(grad_rows).reshape(slots_all, model_width)
        grad_normed = jnp.dot(pick_both, grad_dispatched, preferred_element_type=jnp.float32)
        grad_probs = first_f * gate_first[:, None] + second_f * gate_second[:, None]
        grad_logits = (
            probs_all * (grad_probs - jnp.sum(probs_all * grad_probs, axis=1, keepdims=True))
        ).astype(jnp.bfloat16)
        grads_router.append(contract_rows(normed_two, grad_logits))
        grad_normed = grad_normed + contract_last(grad_logits, router_full[layer_index])
        norm_back = jax.vjp(norm_rows, middle, gains_now[1])[1](grad_normed)
        grad_middle = upstream + norm_back[0]
        grad_branch = grad_middle.astype(jnp.bfloat16)
        grads_out.append(contract_rows(mixed_heads, grad_branch))
        grad_mixed = (
            contract_last(grad_branch, out_full[layer_index])
            .astype(jnp.bfloat16)
            .reshape(images, SEQ, local_heads, HEAD_DIM)
        )
        scores = (
            jnp.einsum("iqhd,ikhd->ihqk", shaped[0], shaped[1], preferred_element_type=jnp.float32)
            * score_scale
        )
        attention_f = jnp.exp(scores - log_total)
        attention = attention_f.astype(jnp.bfloat16)
        grad_value = jnp.einsum(
            "ihqk,iqhd->ikhd", attention, grad_mixed, preferred_element_type=jnp.float32
        ).astype(jnp.bfloat16)
        grad_attention = jnp.einsum(
            "iqhd,ikhd->ihqk", grad_mixed, shaped[2], preferred_element_type=jnp.float32
        )
        grad_scores = (
            attention_f
            * (grad_attention - jnp.sum(attention_f * grad_attention, axis=-1, keepdims=True))
        ).astype(jnp.bfloat16)
        grad_query = (
            jnp.einsum(
                "ihqk,ikhd->iqhd", grad_scores, shaped[1], preferred_element_type=jnp.float32
            )
            * score_scale
        ).astype(jnp.bfloat16)
        grad_key = (
            jnp.einsum(
                "ihqk,iqhd->ikhd", grad_scores, shaped[0], preferred_element_type=jnp.float32
            )
            * score_scale
        ).astype(jnp.bfloat16)
        grad_triple = jnp.stack([grad_query, grad_key, grad_value]).reshape(3, tokens, -1)
        grads_in.append(
            jnp.einsum("td,jth->jdh", normed, grad_triple, preferred_element_type=jnp.float32)
        )
        project = in_full[layer_index]
        grad_normed_one = heads_total(
            jnp.einsum("jth,jdh->td", grad_triple, project, preferred_element_type=jnp.float32)
        )
        norm_back_one = jax.vjp(norm_rows, stream_in, gains_now[0])[1](grad_normed_one)
        grads_gain.append(jnp.stack([norm_back_one[1], norm_back[1]]))
        upstream = grad_middle + norm_back_one[0]
    in_grad_all = jnp.stack(grads_in[::-1])
    out_grad_all = jnp.stack(grads_out[::-1])
    router_grad_all = jnp.stack(grads_router[::-1])
    gain_grad_all = jnp.stack(grads_gain[::-1])
    reduced = (
        lax.psum_scatter(in_grad_all, "expert", scatter_dimension=2, tiled=True),
        lax.psum_scatter(out_grad_all, "expert", scatter_dimension=2, tiled=True),
        lax.psum_scatter(router_grad_all, "expert", scatter_dimension=2, tiled=True),
        lax.psum_scatter(gain_grad_all, "expert", scatter_dimension=2, tiled=True),
    )
    win_grad_all = jnp.stack(grads_win[::-1])[:, None]
    wout_grad_all = jnp.stack(grads_wout[::-1])[:, None]
    return (
        stream,
        upstream,
        reduced[0],
        reduced[1],
        reduced[2],
        reduced[3],
        win_grad_all,
        wout_grad_all,
    )


def solution(mesh):
    placed = (
        P("expert", None),
        P("expert", None),
        P(None, "expert", None),
        P(None, "expert"),
        P(None, None, "expert", "tensor"),
        P(None, "tensor", "expert"),
        P(None, None, "expert"),
        P(None, None, "expert"),
        P(None, "expert", None, "tensor"),
        P(None, "expert", "tensor", None),
    )
    return jax.shard_map(
        local,
        mesh=mesh,
        in_specs=placed,
        out_specs=(
            P("expert", None),
            P("expert", None),
            P(None, None, "expert", "tensor"),
            P(None, "tensor", "expert"),
            P(None, None, "expert"),
            P(None, None, "expert"),
            P(None, "expert", None, "tensor"),
            P(None, "expert", "tensor", None),
        ),
        check_vma=False,
    )
```

profile of v0, /device:TPU:0, one launch (start us, length us, event | category | flops | bytes accessed | tf_op | source)
XLA Modules:
  0.0 1557.0 jit_solution(12436539425469895753)
XLA Ops:
  10.5 10.8 all_gather.26
  21.3 9.3 all_gather.24
  30.9 9.4 all_gather.25
  40.4 6.5 slice_reduce_fusion.8
  68.5 78.9 %all-reduce.10.cloned.1.call-done = f32[985,512]{1,0:T(8,128)} async-done(((f32[985,512]{1,0:T(8,128)}), f32[985,512]{1,0:T(8,128)}) %all-reduce.10.cloned.1.call-update) | async-done | bytes 2017296 | tf_op jit(solution)/shard_map/psum | solution.py:33
  151.9 4.0 fusion.41
  158.1 4.8 all-to-all-start
  166.4 28.0 %all-to-all-done = bf16[8,308,512]{2,1,0:T(8,128)(2,1)} async-done(((bf16[8,308,512]{2,1,0:T(8,128)(2,1)}), bf16[8,308,512]{2,1,0:T(8,128)(2,1)}, u32[]{:S(2)}, u32[]{:S(2)}) %all-to-all-start) | async-done | bytes 2523168 | tf_op jit(solution)/shard_map/all_to_all | solution.py:37
  194.5 4.1 reshape.431
  198.6 5.7 multiply_convert_fusion.1
  207.0 4.8 fusion.106
  211.9 89.2 %reduce-scatter.8.cloned.1.call-done = f32[8,308,128]{2,1,0:T(8,128)} async-done(((f32[8,308,512]{2,1,0:T(8,128)}), f32[8,308,128]{2,1,0:T(8,128)}) %reduce-scatter.8.cloned.1.call-update) | async-done | bytes 1261584 | tf_op jit(solution)/shard_map/reduce_scatter | solution.py:43
  302.5 14.6 all_to_all.40
  317.6 8.0 all_gather.27
  327.9 18.5 %gather_fusion = f32[1970]{0:T(1024)S(1)} fusion(f32[985,8]{0,1:T(8,128)S(1)} %fusion.144, s32[1970]{0:T(1024)S(1)} %reshape.507), kind=kCustom, calls=%fused_computation.clone | custom fusion | bytes 31520 | tf_op jit(solution)/shard_map/jit(take_along_axis)/gather | solution.py:123
  347.5 22.3 %all-gather.5.cloned.1.call-done = bf16[8,308,512]{2,1,0:T(8,128)(2,1)} async-done(((bf16[8,308,128]{2,1,0:T(8,128)(2,1)}), bf16[8,308,512]{2,1,0:T(8,128)(2,1)}) %all-gather.5.cloned.1.call-update) | async-done | bytes 2523152 | tf_op jit(solution)/shard_map/all_gather | solution.py:47
  375.4 6.7 fusion.176
  402.9 78.0 %all-reduce.12.cloned.1.call-done = f32[985,512]{1,0:T(8,128)} async-done(((f32[985,512]{1,0:T(8,128)}), f32[985,512]{1,0:T(8,128)}) %all-reduce.12.cloned.1.call-update) | async-done | bytes 2017296 | tf_op jit(solution)/shard_map/psum | solution.py:33
  485.3 5.5 fusion.38
  493.5 35.3 %all_to_all.41 = bf16[8,308,512]{2,1,0:T(8,128)(2,1)} all-to-all(bf16[8,308,512]{2,1,0:T(8,128)(2,1)S(1)} %reshape.434), channel_id=1, replica_groups=mesh['expert'=8,'tensor'=4] {'expert'}, dimensions={0} | all-to-all | bytes 5046272 | tf_op jit(solution)/shard_map/all_to_all | solution.py:37
  528.8 4.2 reshape.435
  533.1 5.6 multiply_convert_fusion
  541.3 4.8 fusion.104
  546.2 89.0 %reduce-scatter.10.cloned.1.call-done = f32[8,308,128]{2,1,0:T(8,128)} async-done(((f32[8,308,512]{2,1,0:T(8,128)}), f32[8,308,128]{2,1,0:T(8,128)}) %reduce-scatter.10.cloned.1.call-update) | async-done | bytes 1261584 | tf_op jit(solution)/shard_map/reduce_scatter | solution.py:43
  636.6 14.6 all_to_all.42
  653.7 10.0 scatter_custom_fusion.1
  663.7 10.0 scatter_custom_fusion
  676.1 27.8 %all-gather.7.cloned.1.call-done = bf16[8,308,512]{2,1,0:T(8,128)(2,1)} async-done(((bf16[8,308,128]{2,1,0:T(8,128)(2,1)}), bf16[8,308,512]{2,1,0:T(8,128)(2,1)}) %all-gather.7.cloned.1.call-update) | async-done | bytes 2523152 | tf_op jit(solution)/shard_map/all_gather | solution.py:47
  703.8 4.5 reshape.436
  708.4 4.7 fusion
  713.1 4.3 multiply_reduce_fusion.13
  718.1 18.5 %gather_fusion.1 = f32[1970]{0:T(1024)S(1)} fusion(f32[985,8]{0,1:T(8,128)S(1)} %get-tuple-element.98, s32[1970]{0:T(1024)S(1)} %reshape.512), kind=kCustom, calls=%fused_computation.2.clone | custom fusion | bytes 31520 | tf_op jit(solution)/shard_map/jit(take_along_axis)/gather | solution.py:123
  739.3 9.0 concatenate.52
  748.3 8.2 gather_fusion.2
  756.5 3.6 select_convert_fusion.1
  762.8 35.0 %all_to_all.43 = bf16[8,308,512]{2,1,0:T(8,128)(2,1)} all-to-all(bf16[8,308,512]{2,1,0:T(8,128)(2,1)S(1)} %reshape.437), channel_id=1, replica_groups=mesh['expert'=8,'tensor'=4] {'expert'}, dimensions={0} | all-to-all | bytes 5046272 | tf_op jit(solution)/shard_map/all_to_all | solution.py:37
  797.9 4.2 reshape.438
  802.1 6.4 add_convert_fusion.1
  811.2 4.9 fusion.102
  816.2 89.2 %reduce-scatter.12.cloned.1.call-done = f32[8,308,128]{2,1,0:T(8,128)} async-done(((f32[8,308,512]{2,1,0:T(8,128)}), f32[8,308,128]{2,1,0:T(8,128)}) %reduce-scatter.12.cloned.1.call-update) | async-done | bytes 1261584 | tf_op jit(solution)/shard_map/reduce_scatter | solution.py:43
  906.8 14.5 all_to_all.44
  921.5 52.5 %all-gather.9.cloned.1.call-done = bf16[8,308,512]{2,1,0:T(8,128)(2,1)} async-done(((bf16[8,308,128]{2,1,0:T(8,128)(2,1)}), bf16[8,308,512]{2,1,0:T(8,128)(2,1)}) %all-gather.9.cloned.1.call-update) | async-done | bytes 2523152 | tf_op jit(solution)/shard_map/all_gather | solution.py:47
  976.8 2.8 fusion.22
  999.3 82.0 %all-reduce.14.cloned.1.call-done = f32[985,512]{1,0:T(8,128)} async-done(((f32[985,512]{1,0:T(8,128)}), f32[985,512]{1,0:T(8,128)}) %all-reduce.14.cloned.1.call-update) | async-done | bytes 2017296 | tf_op jit(solution)/shard_map/psum | solution.py:33
  1088.9 8.7 concatenate.54
  1097.6 8.2 gather_fusion.3
  1105.8 3.7 select_convert_fusion
  1112.2 35.0 %all_to_all.45 = bf16[8,308,512]{2,1,0:T(8,128)(2,1)} all-to-all(bf16[8,308,512]{2,1,0:T(8,128)(2,1)S(1)} %reshape.441), channel_id=1, replica_groups=mesh['expert'=8,'tensor'=4] {'expert'}, dimensions={0} | all-to-all | bytes 5046272 | tf_op jit(solution)/shard_map/all_to_all | solution.py:37
  1147.2 4.3 reshape.442
  1151.5 6.5 add_convert_fusion
  1160.6 4.9 fusion.100
  1165.6 89.0 %reduce-scatter.14.cloned.1.call-done = f32[8,308,128]{2,1,0:T(8,128)} async-done(((f32[8,308,512]{2,1,0:T(8,128)}), f32[8,308,128]{2,1,0:T(8,128)}) %reduce-scatter.14.cloned.1.call-update) | async-done | bytes 1261584 | tf_op jit(solution)/shard_map/reduce_scatter | solution.py:43
  1255.9 14.5 all_to_all.46
  1275.6 47.4 %all-gather.11.cloned.1.call-done = bf16[8,308,512]{2,1,0:T(8,128)(2,1)} async-done(((bf16[8,308,128]{2,1,0:T(8,128)(2,1)}), bf16[8,308,512]{2,1,0:T(8,128)(2,1)}) %all-gather.11.cloned.1.call-update) | async-done | bytes 2523152 | tf_op jit(solution)/shard_map/all_gather | solution.py:47
  1323.1 4.5 reshape.443
  1327.6 4.7 fusion.17
  1360.2 3.8 copy.354
  1364.2 5.2 convolution_bitcast_fusion.2
  1374.4 24.3 %all-reduce.2 = f32[2,512,8]{1,0,2:T(2,128)S(1)} all-reduce(f32[2,512,8]{1,0,2:T(2,128)S(1)} %copy.356), channel_id=8, replica_groups=mesh['expert'=8,'tensor'=4] {'expert'}, use_global_device_ids=true, to_apply=%region_50.53.clone | all-reduce | flops 8192 | bytes 65536
  1399.9 4.2 convolution_bitcast_fusion.5
  1409.6 14.9 all-reduce.18.cloned.1.call-done
  1427.7 82.3 %all-reduce.16.cloned.1.call-done = f32[985,512]{1,0:T(8,128)} async-done(((f32[985,512]{1,0:T(8,128)}), f32[985,512]{1,0:T(8,128)}) %all-reduce.16.cloned.1.call-update) | async-done | bytes 2017296 | tf_op jit(solution)/shard_map/psum | solution.py:33
  1515.9 3.7 add_add_fusion.4
  1519.6 29.1 %reduce-scatter.16.cloned.1.call-done = f32[64,4]{1,0:T(8,128)} async-done(((f32[512,4]{1,0:T(8,128)}), f32[64,4]{1,0:T(8,128)}) %reduce-scatter.16.cloned.1.call-update) | async-done | bytes 1040
  (590 shorter events, 185.9 us)
Async XLA Ops:
  7.2 140.2 %all-reduce.10.cloned.1.call-start = ((), (), s32[]{:S(2)}) async-start(), calls=%async_computation.13 | async-start | bytes 4063232 | tf_op jit(solution)/shard_map/psum | solution.py:33
  9.9 37.0 %copy-start.99 = (f32[985]{0:T(1024)}, f32[985]{0:T(1024)S(1)}, u32[]{:S(2)}) copy-start(f32[985]{0:T(1024)S(1)} %broadcast_multiply_fusion.7) | copy-start | bytes 11824
  10.3 36.5 %copy-start.127 = (f32[985]{0:T(1024)}, f32[985]{0:T(1024)S(1)}, u32[]{:S(2)}) copy-start(f32[985]{0:T(1024)S(1)} %multiply_reduce_fusion.17) | copy-start | bytes 11824
  10.3 36.5 %copy-start.118 = (f32[985]{0:T(1024)}, f32[985]{0:T(1024)S(1)}, u32[]{:S(2)}) copy-start(f32[985]{0:T(1024)S(1)} %fusion.156) | copy-start | bytes 11824
  21.3 39.8 %copy-start.65 = (bf16[2,128,512]{1,2,0:T(8,128)(2,1)}, bf16[2,128,512]{1,2,0:T(8,128)(2,1)S(1)}, u32[]{:S(2)}) copy-start(bf16[2,128,512]{1,2,0:T(8,128)(2,1)S(1)} %all_gather.26) | copy-start | bytes 786436
  46.9 103.7 %copy-start.142 = (f32[512]{0:T(512)}, f32[512]{0:T(512)S(1)}, u32[]{:S(2)}) copy-start(f32[512]{0:T(512)S(1)} %get-tuple-element.149) | copy-start | bytes 6148
  50.2 8.5 copy-start.43
  68.5 82.6 %copy-start.158 = (s32[985]{0:T(1024)}, s32[985]{0:T(1024)S(1)}, u32[]{:S(2)}) copy-start(s32[985]{0:T(1024)S(1)} %get-tuple-element.78) | copy-start | bytes 11824
  68.5 82.6 %copy-start.161 = (s32[985]{0:T(1024)}, s32[985]{0:T(1024)S(1)}, u32[]{:S(2)}) copy-start(s32[985]{0:T(1024)S(1)} %get-tuple-element.79) | copy-start | bytes 11824
  158.1 36.3 %all-to-all-start = ((bf16[8,308,512]{2,1,0:T(8,128)(2,1)}), bf16[8,308,512]{2,1,0:T(8,128)(2,1)}, u32[]{:S(2)}, u32[]{:S(2)}) async-start(bf16[8,308,512]{2,1,0:T(8,128)(2,1)} %reshape.430), calls=%async_computation | async-start | bytes 5111808 | tf_op jit(solution)/shard_map/all_to_all | solution.py:37
  162.9 138.1 %reduce-scatter.8.cloned.1.call-start = ((), (), s32[]{:S(2)}) async-start(), calls=%async_computation.14 | async-start | bytes 6389760 | tf_op jit(solution)/shard_map/reduce_scatter | solution.py:43
  165.2 33.4 %copy-start.31 = (bf16[2,1,512,512]{3,2,1,0:T(8,128)(2,1)}, bf16[2,1,512,512]{3,2,1,0:T(8,128)(2,1)S(1)}, u32[]{:S(2)}) copy-start(bf16[2,1,512,512]{3,2,1,0:T(8,128)(2,1)S(1)} %convert.8) | copy-start | bytes 3145732
  211.9 105.3 %copy-start.170 = (f32[2,512,1]{1,2,0:T(1,128)S(1)}, f32[2,512,1]{1,2,0:T(1,128)}, u32[]{:S(2)}) copy-start(f32[2,512,1]{1,2,0:T(1,128)} %param.20) | copy-start | bytes 12292
  211.9 157.9 %all-gather.5.cloned.1.call-start = ((), (), s32[]{:S(2)}) async-start(), calls=%async_computation.15 | async-start | bytes 3194880 | tf_op jit(solution)/shard_map/all_gather | solution.py:47
  302.5 23.8 %copy-start.22 = (bf16[985,512]{1,0:T(8,128)(2,1)S(1)}, bf16[985,512]{1,0:T(8,128)(2,1)}, u32[]{:S(2)}) copy-start(bf16[985,512]{1,0:T(8,128)(2,1)} %copy-done.21) | copy-start | bytes 3025924
  317.1 163.8 %all-reduce.12.cloned.1.call-start = ((), (), s32[]{:S(2)}) async-start(), calls=%async_computation.16 | async-start | bytes 4063232 | tf_op jit(solution)/shard_map/psum | solution.py:33
  347.4 27.9 %copy-start.152 = (f32[985]{0:T(1024)}, f32[985]{0:T(1024)S(1)}, u32[]{:S(2)}) copy-start(f32[985]{0:T(1024)S(1)} %get-tuple-element.76) | copy-start | bytes 11824
  347.4 27.9 %copy-start.154 = (f32[985]{0:T(1024)}, f32[985]{0:T(1024)S(1)}, u32[]{:S(2)}) copy-start(f32[985]{0:T(1024)S(1)} %get-tuple-element.77) | copy-start | bytes 11824
  347.4 25.0 %copy-start.159 = (s32[985]{0:T(1024)S(1)}, s32[985]{0:T(1024)}, u32[]{:S(2)}) copy-start(s32[985]{0:T(1024)} %copy-done.158) | copy-start | bytes 11824
  382.1 98.8 %copy-start.9 = (f32[985,512]{1,0:T(8,128)}, f32[985,512]{1,0:T(8,128)S(1)}, u32[]{:S(2)}) copy-start(f32[985,512]{1,0:T(8,128)S(1)} %get-tuple-element.102) | copy-start | bytes 6051844
  398.5 236.7 %reduce-scatter.10.cloned.1.call-start = ((), (), s32[]{:S(2)}) async-start(), calls=%async_computation.17 | async-start | bytes 6389760 | tf_op jit(solution)/shard_map/reduce_scatter | solution.py:43
  398.8 252.6 %copy-start.17 = (s32[1,985,2]{2,1,0:T(8,128)}, s32[1,985,2]{2,1,0:T(8,128)S(1)}, u32[]{:S(2)}) copy-start(s32[1,985,2]{2,1,0:T(8,128)S(1)} %copy.402) | copy-start | bytes 23644
  402.9 81.7 %copy-start.164 = (s32[985]{0:T(1024)}, s32[985]{0:T(1024)S(1)}, u32[]{:S(2)}) copy-start(s32[985]{0:T(1024)S(1)} %get-tuple-element.72) | copy-start | bytes 11824
  402.9 81.7 %copy-start.167 = (s32[985]{0:T(1024)}, s32[985]{0:T(1024)S(1)}, u32[]{:S(2)}) copy-start(s32[985]{0:T(1024)S(1)} %get-tuple-element.73) | copy-start | bytes 11824
  546.1 157.7 %all-gather.7.cloned.1.call-start = ((), (), s32[]{:S(2)}) async-start(), calls=%async_computation.18 | async-start | bytes 3194880 | tf_op jit(solution)/shard_map/all_gather | solution.py:47
  636.6 15.2 copy-start.74
  636.6 15.4 copy-start.73
  651.2 23.7 %copy-start.25 = (bf16[985,512]{1,0:T(8,128)(2,1)S(1)}, bf16[985,512]{1,0:T(8,128)(2,1)}, u32[]{:S(2)}) copy-start(bf16[985,512]{1,0:T(8,128)(2,1)} %copy-done.24) | copy-start | bytes 3025924
  651.3 254.1 %reduce-scatter.12.cloned.1.call-start = ((), (), s32[]{:S(2)}) async-start(), calls=%async_computation.19 | async-start | bytes 6389760 | tf_op jit(solution)/shard_map/reduce_scatter | solution.py:43
  663.6 44.7 %copy-start.91 = (s32[2465]{0:T(1024)}, s32[2465]{0:T(1024)S(1)}, u32[]{:S(2)}) copy-start(s32[2465]{0:T(1024)S(1)} %scatter_custom_fusion.1) | copy-start | bytes 29584
  676.1 32.3 %copy-start.168 = (s32[985]{0:T(1024)S(1)}, s32[985]{0:T(1024)}, u32[]{:S(2)}) copy-start(s32[985]{0:T(1024)} %copy-done.167) | copy-start | bytes 11824
  718.1 18.9 %copy-start.18 = (s32[1,985,2]{2,1,0:T(8,128)S(1)}, s32[1,985,2]{2,1,0:T(8,128)}, u32[]{:S(2)}) copy-start(s32[1,985,2]{2,1,0:T(8,128)} %copy-done.17) | copy-start | bytes 23644
  739.3 9.0 copy-start.123
  748.3 8.2 copy-start.156
  816.1 105.3 %copy-start.110 = (s32[985]{0:T(1024)S(1)}, s32[985]{0:T(1024)}, u32[]{:S(2)}) copy-start(s32[985]{0:T(1024)} %copy-done.108) | copy-start | bytes 11824
  816.1 105.3 %copy-start.126 = (s32[985]{0:T(1024)S(1)}, s32[985]{0:T(1024)}, u32[]{:S(2)}) copy-start(s32[985]{0:T(1024)} %copy-done.124) | copy-start | bytes 11824
  816.1 105.3 %copy-start.147 = (f32[985]{0:T(1024)S(1)}, f32[985]{0:T(1024)}, u32[]{:S(2)}) copy-start(f32[985]{0:T(1024)} %copy-done.146) | copy-start | bytes 11824
  816.1 105.3 %copy-start.149 = (f32[985]{0:T(1024)S(1)}, f32[985]{0:T(1024)}, u32[]{:S(2)}) copy-start(f32[985]{0:T(1024)} %copy-done.148) | copy-start | bytes 11824
  816.1 105.3 %copy-start.150 = (f32[985]{0:T(1024)S(1)}, f32[985]{0:T(1024)}, u32[]{:S(2)}) copy-start(f32[985]{0:T(1024)} %get-tuple-element.97) | copy-start | bytes 11824
  816.1 157.8 %all-gather.9.cloned.1.call-start = ((), (), s32[]{:S(2)}) async-start(), calls=%async_computation.20 | async-start | bytes 3194880 | tf_op jit(solution)/shard_map/all_gather | solution.py:47
  921.3 160.1 %all-reduce.14.cloned.1.call-start = ((), (), s32[]{:S(2)}) async-start(), calls=%async_computation.21 | async-start | bytes 4063232 | tf_op jit(solution)/shard_map/psum | solution.py:33
  921.4 55.3 %copy-start.166 = (s32[985]{0:T(1024)S(1)}, s32[985]{0:T(1024)}, u32[]{:S(2)}) copy-start(s32[985]{0:T(1024)} %copy-done.164) | copy-start | bytes 11824
  921.4 55.3 %copy-start.169 = (s32[985]{0:T(1024)S(1)}, s32[985]{0:T(1024)}, u32[]{:S(2)}) copy-start(s32[985]{0:T(1024)} %copy-done.167) | copy-start | bytes 11824
  996.9 84.4 %copy-start.10 = (f32[985,512]{1,0:T(8,128)S(1)}, f32[985,512]{1,0:T(8,128)}, u32[]{:S(2)}) copy-start(f32[985,512]{1,0:T(8,128)} %copy-done.9) | copy-start | bytes 6051844
  997.0 84.4 %copy-start.102 = (f32[985]{0:T(1024)S(1)}, f32[985]{0:T(1024)}, u32[]{:S(2)}) copy-start(f32[985]{0:T(1024)} %copy-done.101) | copy-start | bytes 11824
  997.0 84.4 %copy-start.121 = (f32[985]{0:T(1024)S(1)}, f32[985]{0:T(1024)}, u32[]{:S(2)}) copy-start(f32[985]{0:T(1024)} %copy-done.120) | copy-start | bytes 11824
  997.0 84.4 %copy-start.140 = (f32[512]{0:T(512)S(1)}, f32[512]{0:T(512)}, u32[]{:S(2)}) copy-start(f32[512]{0:T(512)} %get-tuple-element.83) | copy-start | bytes 6148
  999.0 84.8 %copy-start.132 = (f32[985]{0:T(1024)S(1)}, f32[985]{0:T(1024)}, u32[]{:S(2)}) copy-start(f32[985]{0:T(1024)} %copy-done.131) | copy-start | bytes 11824
  999.0 255.5 %reduce-scatter.14.cloned.1.call-start = ((), (), s32[]{:S(2)}) async-start(), calls=%async_computation.22 | async-start | bytes 6389760 | tf_op jit(solution)/shard_map/reduce_scatter | solution.py:43
  1088.9 8.7 copy-start.122
  1165.5 105.0 %copy-start.172 = (u32[32]{0:T(128)S(1)}, u32[32]{0:T(128)}, u32[]{:S(2)}) copy-start(u32[32]{0:T(128)} %constant.118) | copy-start | bytes 388
  1165.5 106.3 %copy-start.26 = (bf16[985,512]{1,0:T(8,128)(2,1)S(1)}, bf16[985,512]{1,0:T(8,128)(2,1)}, u32[]{:S(2)}) copy-start(bf16[985,512]{1,0:T(8,128)(2,1)} %copy-done.24) | copy-start | bytes 3025924
  1165.5 106.5 %copy-start.64 = (bf16[985,128]{0,1:T(8,128)(2,1)S(1)}, bf16[985,128]{0,1:T(8,128)(2,1)}, u32[]{:S(2)}) copy-start(bf16[985,128]{0,1:T(8,128)(2,1)} %copy-done.63) | copy-start | bytes 756484
  1165.5 157.5 %all-gather.11.cloned.1.call-start = ((), (), s32[]{:S(2)}) async-start(), calls=%async_computation.23 | async-start | bytes 3194880 | tf_op jit(solution)/shard_map/all_gather | solution.py:47
  1270.5 154.0 %all-reduce.18.cloned.1.call-start = ((), (), s32[]{:S(2)}) async-start(), calls=%async_computation.26 | async-start | bytes 4194304
  1275.6 52.0 %copy-start.160 = (s32[985]{0:T(1024)S(1)}, s32[985]{0:T(1024)}, u32[]{:S(2)}) copy-start(s32[985]{0:T(1024)} %copy-done.158) | copy-start | bytes 11824
  1275.6 52.0 %copy-start.163 = (s32[985]{0:T(1024)S(1)}, s32[985]{0:T(1024)}, u32[]{:S(2)}) copy-start(s32[985]{0:T(1024)} %copy-done.161) | copy-start | bytes 11824
  1350.1 8.0 copy-start.5
  1350.2 8.0 copy-start.100
  1350.2 8.0 copy-start.119
  1350.2 8.0 copy-start.138
  1364.1 145.9 %all-reduce.16.cloned.1.call-start = ((), (), s32[]{:S(2)}) async-start(), calls=%async_computation.24 | async-start | bytes 4063232 | tf_op jit(solution)/shard_map/psum | solution.py:33
  1374.0 174.7 %reduce-scatter.16.cloned.1.call-start = ((), (), s32[]{:S(2)}) async-start(), calls=%async_computation.25 | async-start | bytes 294912
  1427.7 84.8 %copy-start.128 = (f32[985]{0:T(1024)S(1)}, f32[985]{0:T(1024)}, u32[]{:S(2)}) copy-start(f32[985]{0:T(1024)} %copy-done.127) | copy-start | bytes 11824
  (124 other events, 291.4 us)
Sparse Core Ops, SparseCore 0:
  63.0 84.3 all-reduce.9
  212.0 89.0 reduce-scatter.7
  317.3 52.4 all-gather.4
  398.6 82.2 all-reduce.11
  546.2 88.8 reduce-scatter.9
  651.4 52.4 all-gather.6
  816.2 89.1 reduce-scatter.11
  921.4 52.4 all-gather.8
  999.1 82.1 all-reduce.13
  1165.6 88.8 reduce-scatter.13
  1270.6 52.4 all-gather.10
  1364.2 60.2 all-reduce.17
  1426.9 83.0 all-reduce.15
  1516.0 32.6 reduce-scatter.15
where the time goes:
time: 1570 us; the launch traced here: 1560 us
  waiting for transfers between devices  900 us (57%)
  local copies, waits for them, and re-layouts  233 us (15%)
  blocking collectives  225 us (14%)
  matrix products  122 us (8%)
  other arithmetic  53.5 us (3%)
  between operations  17.5 us (1%)
    reduce_scatter x4, waiting for transfers between devices, to_sources(): lax.psum_scatter(partial_rows, 'tensor', scatter_dimension=2, tiled=True)  356 us
    psum x4, waiting for transfers between devices, heads_total(): return lax.psum(partial_sum, 'tensor')  321 us
    all_gather x4, waiting for transfers between devices, to_sources(): return lax.all_gather(moved, 'tensor', axis=2, tiled=True)  150 us
    all_to_all x3, blocking collectives, to_experts(): lax.all_to_all(make_rows(0, model_width), 'expert', split_axis=0, concat_...  105 us
    all_to_all x4, blocking collectives, to_sources(): lax.all_to_all(shares.astype(jnp.bfloat16), 'expert', split_axis=0, conca...  58.3 us
    unnamed x16, waiting for transfers between devices  44.2 us
    gather x6, local copies, waits for them, and re-layouts, local(): gate_values = jnp.take_along_axis(probs_all, chosen, axis=1)  38.4 us
  transfers between devices with their start and end apart: 15, of which 15 were waited for; matrix products, arithmetic and copies ran while one was open for 6% of the time, Pallas kernels for 0%

commit v1 on v0

--- a/solution.py
+++ b/solution.py
@@ -5,6 +5,7 @@
 
 HEAD_DIM = 64
 SEQ = 197
+sectors_answer = lambda frame_in, along_axis: jnp.sum(jax.lax.all_gather(frame_in, along_axis), 0)
 
 
 def norm_rows(rows_in, gain_row):
@@ -30,7 +31,7 @@
 
 
 def heads_total(partial_sum):
-    return lax.psum(partial_sum, "tensor")
+    return sectors_answer(partial_sum, "tensor")
 
 
 def to_experts(make_rows, model_width):

time: 1570 us -> 1830 us (1.17)
  waiting for transfers between devices: 900 us -> 1130 us
  other arithmetic: 53.5 us -> 81.9 us
    all_gather x0 -> x4, waiting for transfers between devices: none -> 545 us  [jax.lax.all_gather(frame_in, along_axis)]
    psum x4 -> x0, waiting for transfers between devices: 321 us -> none  [heads_total(): return lax.psum(partial_sum, 'tensor')]
    reduce_sum x0 -> x4, other arithmetic: none -> 23.3 us  [jnp.sum(jax.lax.all_gather(frame_in, along_axis), 0)]
  transfers between devices with their start and end apart: 15 -> 15, of which waited for: 15 -> 15; matrix products, arithmetic and copies ran while one was open for 6% -> 5% of each run, Pallas kernels for 0% -> 0%
where the time goes in v1:
time: 1830 us; the launch traced here: 1820 us
  waiting for transfers between devices  1130 us (62%)
  local copies, waits for them, and re-layouts  227 us (12%)
  blocking collectives  225 us (12%)
  matrix products  134 us (7%)
  other arithmetic  81.9 us (4%)
    all_gather x4, waiting for transfers between devices, jax.lax.all_gather(frame_in, along_axis)  545 us
    reduce_scatter x4, waiting for transfers between devices, to_sources(): lax.psum_scatter(partial_rows, 'tensor', scatter_dimension=2, tiled=True)  354 us
    all_gather x4, waiting for transfers between devices, to_sources(): return lax.all_gather(moved, 'tensor', axis=2, tiled=True)  164 us
    all_to_all x3, blocking collectives, to_experts(): lax.all_to_all(make_rows(0, model_width), 'expert', split_axis=0, concat_...  106 us
    all_to_all x4, blocking collectives, to_sources(): lax.all_to_all(shares.astype(jnp.bfloat16), 'expert', split_axis=0, conca...  58.2 us
    unnamed x16, waiting for transfers between devices  41.6 us
    dot_general x10, matrix products, contract_rows(): lax.dot_general(left_side, right_side, (((0,), (0,)), ((), ())), preferre...  39.4 us
    gather x6, local copies, waits for them, and re-layouts, local(): gate_values = jnp.take_along_axis(probs_all, chosen, axis=1)  38.4 us
  transfers between devices with their start and end apart: 15, of which 15 were waited for; matrix products, arithmetic and copies ran while one was open for 5% of the time, Pallas kernels for 0%

profile of v1, /device:TPU:0, one launch (start us, length us, event | category | flops | bytes accessed | tf_op | source)
XLA Modules:
  0.0 1822.7 jit_solution(2289284177472093877)
XLA Ops:
  10.5 10.8 all_gather.50
  21.3 9.3 all_gather.48
  31.0 9.4 all_gather.49
  40.4 6.6 slice_reduce_fusion.8
  81.1 126.2 %all-gather.25.cloned.1.call-done = f32[4,985,512]{2,1,0:T(8,128)} async-done(((f32[1,985,512]{2,1,0:T(8,128)}), f32[4,985,512]{2,1,0:T(8,128)}) %all-gather.25.cloned.1.call-update) | async-done | bytes 8069136 | tf_op jit(solution)/shard_map/all_gather | solution.py:8
  207.3 5.8 reduce_sum.372
  216.3 17.5 fusion.41
  233.8 4.1 reshape.430
  237.9 4.4 all-to-all-start
  246.4 27.5 %all-to-all-done = bf16[8,308,512]{2,1,0:T(8,128)(2,1)} async-done(((bf16[8,308,512]{2,1,0:T(8,128)(2,1)}), bf16[8,308,512]{2,1,0:T(8,128)(2,1)}, u32[]{:S(2)}, u32[]{:S(2)}) %all-to-all-start) | async-done | bytes 2523168 | tf_op jit(solution)/shard_map/all_to_all | solution.py:38
  273.9 4.1 reshape.431
  278.0 5.4 multiply_convert_fusion.1
  283.4 4.1 dot_general.183
  287.6 5.6 fusion.106
  293.3 88.1 %reduce-scatter.8.cloned.1.call-done = f32[8,308,128]{2,1,0:T(8,128)} async-done(((f32[8,308,512]{2,1,0:T(8,128)}), f32[8,308,128]{2,1,0:T(8,128)}) %reduce-scatter.8.cloned.1.call-update) | async-done | bytes 1261584 | tf_op jit(solution)/shard_map/reduce_scatter | solution.py:44
  382.8 14.5 all_to_all.40
  397.9 8.0 all_gather.53
  406.9 18.5 %gather_fusion = f32[1970]{0:T(1024)S(1)} fusion(f32[985,8]{0,1:T(8,128)S(1)} %fusion.142, s32[1970]{0:T(1024)S(1)} %reshape.523), kind=kCustom, calls=%fused_computation.clone | custom fusion | bytes 31520 | tf_op jit(solution)/shard_map/jit(take_along_axis)/gather | solution.py:124
  426.6 23.4 %all-gather.17.cloned.1.call-done = bf16[8,308,512]{2,1,0:T(8,128)(2,1)} async-done(((bf16[8,308,128]{2,1,0:T(8,128)(2,1)}), bf16[8,308,512]{2,1,0:T(8,128)(2,1)}) %all-gather.17.cloned.1.call-update) | async-done | bytes 2523152 | tf_op jit(solution)/shard_map/all_gather | solution.py:48
  455.6 6.7 fusion.174
  476.4 143.6 %all-gather.27.cloned.1.call-done = f32[4,985,512]{2,1,0:T(8,128)} async-done(((f32[1,985,512]{2,1,0:T(8,128)}), f32[4,985,512]{2,1,0:T(8,128)}) %all-gather.27.cloned.1.call-update) | async-done | bytes 8069136 | tf_op jit(solution)/shard_map/all_gather | solution.py:8
  620.0 5.8 reduce_sum.391
  630.3 5.5 fusion.38
  638.4 35.0 %all_to_all.41 = bf16[8,308,512]{2,1,0:T(8,128)(2,1)} all-to-all(bf16[8,308,512]{2,1,0:T(8,128)(2,1)S(1)} %reshape.434), channel_id=1, replica_groups=mesh['expert'=8,'tensor'=4] {'expert'}, dimensions={0} | all-to-all | bytes 5046272 | tf_op jit(solution)/shard_map/all_to_all | solution.py:38
  673.5 4.2 reshape.435
  677.7 5.7 multiply_convert_fusion
  686.1 4.7 fusion.104
  690.9 88.1 %reduce-scatter.10.cloned.1.call-done = f32[8,308,128]{2,1,0:T(8,128)} async-done(((f32[8,308,512]{2,1,0:T(8,128)}), f32[8,308,128]{2,1,0:T(8,128)}) %reduce-scatter.10.cloned.1.call-update) | async-done | bytes 1261584 | tf_op jit(solution)/shard_map/reduce_scatter | solution.py:44
  780.5 14.6 all_to_all.42
  796.3 10.0 scatter_custom_fusion
  807.9 39.8 %all-gather.19.cloned.1.call-done = bf16[8,308,512]{2,1,0:T(8,128)(2,1)} async-done(((bf16[8,308,128]{2,1,0:T(8,128)(2,1)}), bf16[8,308,512]{2,1,0:T(8,128)(2,1)}) %all-gather.19.cloned.1.call-update) | async-done | bytes 2523152 | tf_op jit(solution)/shard_map/all_gather | solution.py:48
  847.8 4.1 reshape.436
  851.9 4.7 fusion
  856.6 4.4 multiply_reduce_fusion.13
  861.6 18.5 %gather_fusion.1 = f32[1970]{0:T(1024)S(1)} fusion(f32[985,8]{0,1:T(8,128)S(1)} %get-tuple-element.98, s32[1970]{0:T(1024)S(1)} %reshape.528), kind=kCustom, calls=%fused_computation.2.clone | custom fusion | bytes 31520 | tf_op jit(solution)/shard_map/jit(take_along_axis)/gather | solution.py:124
  882.9 9.0 concatenate.52
  891.8 8.2 gather_fusion.2
  906.3 35.5 %all_to_all.43 = bf16[8,308,512]{2,1,0:T(8,128)(2,1)} all-to-all(bf16[8,308,512]{2,1,0:T(8,128)(2,1)S(1)} %reshape.437), channel_id=1, replica_groups=mesh['expert'=8,'tensor'=4] {'expert'}, dimensions={0} | all-to-all | bytes 5046272 | tf_op jit(solution)/shard_map/all_to_all | solution.py:38
  941.8 4.3 reshape.438
  946.1 6.5 add_convert_fusion.1
  955.2 4.8 fusion.102
  960.1 89.3 %reduce-scatter.12.cloned.1.call-done = f32[8,308,128]{2,1,0:T(8,128)} async-done(((f32[8,308,512]{2,1,0:T(8,128)}), f32[8,308,128]{2,1,0:T(8,128)}) %reduce-scatter.12.cloned.1.call-update) | async-done | bytes 1261584 | tf_op jit(solution)/shard_map/reduce_scatter | solution.py:44
  1050.8 14.5 all_to_all.44
  1065.4 52.5 %all-gather.21.cloned.1.call-done = bf16[8,308,512]{2,1,0:T(8,128)(2,1)} async-done(((bf16[8,308,128]{2,1,0:T(8,128)(2,1)}), bf16[8,308,512]{2,1,0:T(8,128)(2,1)}) %all-gather.21.cloned.1.call-update) | async-done | bytes 2523152 | tf_op jit(solution)/shard_map/all_gather | solution.py:48
  1143.3 10.0 scatter_custom_fusion.1
  1153.3 132.3 %all-gather.29.cloned.1.call-done = f32[4,985,512]{2,1,0:T(8,128)} async-done(((f32[1,985,512]{2,1,0:T(8,128)}), f32[4,985,512]{2,1,0:T(8,128)}) %all-gather.29.cloned.1.call-update) | async-done | bytes 8069136 | tf_op jit(solution)/shard_map/all_gather | solution.py:8
  1285.7 5.8 reduce_sum.413
  1299.4 8.9 concatenate.54
  1308.4 8.2 gather_fusion.3
  1322.8 35.0 %all_to_all.45 = bf16[8,308,512]{2,1,0:T(8,128)(2,1)} all-to-all(bf16[8,308,512]{2,1,0:T(8,128)(2,1)S(1)} %reshape.441), channel_id=1, replica_groups=mesh['expert'=8,'tensor'=4] {'expert'}, dimensions={0} | all-to-all | bytes 5046272 | tf_op jit(solution)/shard_map/all_to_all | solution.py:38
  1357.9 4.2 reshape.442
  1362.1 6.5 add_convert_fusion
  1371.2 4.9 fusion.100
  1376.2 88.1 %reduce-scatter.14.cloned.1.call-done = f32[8,308,128]{2,1,0:T(8,128)} async-done(((f32[8,308,512]{2,1,0:T(8,128)}), f32[8,308,128]{2,1,0:T(8,128)}) %reduce-scatter.14.cloned.1.call-update) | async-done | bytes 1261584 | tf_op jit(solution)/shard_map/reduce_scatter | solution.py:44
  1465.7 14.6 all_to_all.46
  1485.1 47.9 %all-gather.23.cloned.1.call-done = bf16[8,308,512]{2,1,0:T(8,128)(2,1)} async-done(((bf16[8,308,128]{2,1,0:T(8,128)(2,1)}), bf16[8,308,512]{2,1,0:T(8,128)(2,1)}) %all-gather.23.cloned.1.call-update) | async-done | bytes 2523152 | tf_op jit(solution)/shard_map/all_gather | solution.py:48
  1569.2 4.2 convolution_bitcast_fusion.4
  1576.2 24.2 %all-reduce.2 = f32[2,512,8]{1,0,2:T(2,128)S(1)} all-reduce(f32[2,512,8]{1,0,2:T(2,128)S(1)} %copy.356), channel_id=12, replica_groups=mesh['expert'=8,'tensor'=4] {'expert'}, use_global_device_ids=true, to_apply=%region_50.53.clone | all-reduce | flops 8192 | bytes 65536
  1601.7 4.2 convolution_bitcast_fusion.7
  1611.5 13.0 all-reduce.6.cloned.1.call-done
  1627.6 142.8 %all-gather.31.cloned.1.call-done = f32[4,985,512]{2,1,0:T(8,128)} async-done(((f32[1,985,512]{2,1,0:T(8,128)}), f32[4,985,512]{2,1,0:T(8,128)}) %all-gather.31.cloned.1.call-update) | async-done | bytes 8069136 | tf_op jit(solution)/shard_map/all_gather | solution.py:8
  1770.5 5.9 reduce_sum.428
  1782.2 3.7 add_add_fusion.4
  1785.9 28.3 %reduce-scatter.16.cloned.1.call-done = f32[64,4]{1,0:T(8,128)} async-done(((f32[512,4]{1,0:T(8,128)}), f32[64,4]{1,0:T(8,128)}) %reduce-scatter.16.cloned.1.call-update) | async-done | bytes 1040
  (578 shorter events, 198.9 us)
Async XLA Ops:
  7.2 200.2 %all-gather.25.cloned.1.call-start = ((), (), s32[]{:S(2)}) async-start(), calls=%async_computation.21 | async-start | bytes 10158080 | tf_op jit(solution)/shard_map/all_gather | solution.py:8
  9.9 37.1 %copy-start.92 = (f32[985]{0:T(1024)}, f32[985]{0:T(1024)S(1)}, u32[]{:S(2)}) copy-start(f32[985]{0:T(1024)S(1)} %broadcast_multiply_fusion.7) | copy-start | bytes 11824
  10.3 11.0 copy-start.120
  10.3 37.5 %copy-start.112 = (f32[985]{0:T(1024)}, f32[985]{0:T(1024)S(1)}, u32[]{:S(2)}) copy-start(f32[985]{0:T(1024)S(1)} %fusion.154) | copy-start | bytes 11824
  21.3 38.4 %copy-start.61 = (bf16[2,128,512]{1,2,0:T(8,128)(2,1)}, bf16[2,128,512]{1,2,0:T(8,128)(2,1)S(1)}, u32[]{:S(2)}) copy-start(bf16[2,128,512]{1,2,0:T(8,128)(2,1)S(1)} %all_gather.50) | copy-start | bytes 786436
  40.4 7.4 copy-start.35
  50.1 7.7 copy-start.39
  62.4 14.3 copy-start.17
  81.1 135.2 %copy-start.154 = (s32[985]{0:T(1024)}, s32[985]{0:T(1024)S(1)}, u32[]{:S(2)}) copy-start(s32[985]{0:T(1024)S(1)} %get-tuple-element.152) | copy-start | bytes 11824
  81.1 135.2 %copy-start.157 = (s32[985]{0:T(1024)}, s32[985]{0:T(1024)S(1)}, u32[]{:S(2)}) copy-start(s32[985]{0:T(1024)S(1)} %get-tuple-element.153) | copy-start | bytes 11824
  215.5 18.3 %copy-start.122 = (f32[985]{0:T(1024)}, f32[985]{0:T(1024)S(1)}, u32[]{:S(2)}) copy-start(f32[985]{0:T(1024)S(1)} %multiply_reduce_fusion.16) | copy-start | bytes 11824
  215.5 18.3 %copy-start.110 = (f32[985]{0:T(1024)}, f32[985]{0:T(1024)S(1)}, u32[]{:S(2)}) copy-start(f32[985]{0:T(1024)S(1)} %fusion.155) | copy-start | bytes 11824
  216.3 190.2 %copy-start.24 = (bf16[985,512]{1,0:T(8,128)(2,1)}, bf16[985,512]{1,0:T(8,128)(2,1)S(1)}, u32[]{:S(2)}) copy-start(bf16[985,512]{1,0:T(8,128)(2,1)S(1)} %multiply_convert_fusion.6) | copy-start | bytes 3025924
  237.9 36.0 %all-to-all-start = ((bf16[8,308,512]{2,1,0:T(8,128)(2,1)}), bf16[8,308,512]{2,1,0:T(8,128)(2,1)}, u32[]{:S(2)}, u32[]{:S(2)}) async-start(bf16[8,308,512]{2,1,0:T(8,128)(2,1)} %reshape.430), calls=%async_computation | async-start | bytes 5111808 | tf_op jit(solution)/shard_map/all_to_all | solution.py:38
  242.3 139.1 %reduce-scatter.8.cloned.1.call-start = ((), (), s32[]{:S(2)}) async-start(), calls=%async_computation.13 | async-start | bytes 6389760 | tf_op jit(solution)/shard_map/reduce_scatter | solution.py:44
  293.2 104.2 %copy-start.152 = (f32[2,512,1]{1,2,0:T(1,128)S(1)}, f32[2,512,1]{1,2,0:T(1,128)}, u32[]{:S(2)}) copy-start(f32[2,512,1]{1,2,0:T(1,128)} %param.20) | copy-start | bytes 12292
  293.2 156.7 %all-gather.17.cloned.1.call-start = ((), (), s32[]{:S(2)}) async-start(), calls=%async_computation.14 | async-start | bytes 3194880 | tf_op jit(solution)/shard_map/all_gather | solution.py:48
  397.3 222.7 %all-gather.27.cloned.1.call-start = ((), (), s32[]{:S(2)}) async-start(), calls=%async_computation.22 | async-start | bytes 10158080 | tf_op jit(solution)/shard_map/all_gather | solution.py:8
  406.5 19.0 %copy-start.98 = (bf16[1,512,8]{1,0,2:T(2,128)(2,1)}, bf16[1,512,8]{1,0,2:T(2,128)(2,1)S(1)}, u32[]{:S(2)}) copy-start(bf16[1,512,8]{1,0,2:T(2,128)(2,1)S(1)} %get-tuple-element.123) | copy-start | bytes 24580
  406.8 18.6 %copy-start.79 = (f32[985,8]{0,1:T(8,128)}, f32[985,8]{0,1:T(8,128)S(1)}, u32[]{:S(2)}) copy-start(f32[985,8]{0,1:T(8,128)S(1)} %get-tuple-element.133) | copy-start | bytes 94564
  406.9 18.6 %copy-start.88 = (f32[985]{0:T(1024)}, f32[985]{0:T(1024)S(1)}, u32[]{:S(2)}) copy-start(f32[985]{0:T(1024)S(1)} %get-tuple-element.132) | copy-start | bytes 11824
  406.9 18.6 %copy-start.108 = (f32[985]{0:T(1024)}, f32[985]{0:T(1024)S(1)}, u32[]{:S(2)}) copy-start(f32[985]{0:T(1024)S(1)} %fusion.143) | copy-start | bytes 11824
  426.5 29.0 %copy-start.146 = (f32[985]{0:T(1024)}, f32[985]{0:T(1024)S(1)}, u32[]{:S(2)}) copy-start(f32[985]{0:T(1024)S(1)} %get-tuple-element.76) | copy-start | bytes 11824
  426.6 29.0 %copy-start.148 = (f32[985]{0:T(1024)}, f32[985]{0:T(1024)S(1)}, u32[]{:S(2)}) copy-start(f32[985]{0:T(1024)S(1)} %get-tuple-element.77) | copy-start | bytes 11824
  426.6 26.1 %copy-start.158 = (s32[985]{0:T(1024)S(1)}, s32[985]{0:T(1024)}, u32[]{:S(2)}) copy-start(s32[985]{0:T(1024)} %copy-done.157) | copy-start | bytes 11824
  455.5 6.8 copy-start.66
  462.3 163.6 %copy-start.9 = (f32[985,512]{1,0:T(8,128)}, f32[985,512]{1,0:T(8,128)S(1)}, u32[]{:S(2)}) copy-start(f32[985,512]{1,0:T(8,128)S(1)} %get-tuple-element.102) | copy-start | bytes 6051844
  476.4 302.7 %reduce-scatter.10.cloned.1.call-start = ((), (), s32[]{:S(2)}) async-start(), calls=%async_computation.15 | async-start | bytes 6389760 | tf_op jit(solution)/shard_map/reduce_scatter | solution.py:44
  690.9 104.5 %copy-start.18 = (s32[1,985,2]{2,1,0:T(8,128)S(1)}, s32[1,985,2]{2,1,0:T(8,128)}, u32[]{:S(2)}) copy-start(s32[1,985,2]{2,1,0:T(8,128)} %copy-done.17) | copy-start | bytes 23644
  690.9 156.9 %all-gather.19.cloned.1.call-start = ((), (), s32[]{:S(2)}) async-start(), calls=%async_computation.16 | async-start | bytes 3194880 | tf_op jit(solution)/shard_map/all_gather | solution.py:48
  780.4 15.4 copy-start.75
  780.5 15.6 copy-start.74
  780.5 27.0 %copy-start.27 = (bf16[985,512]{1,0:T(8,128)(2,1)S(1)}, bf16[985,512]{1,0:T(8,128)(2,1)}, u32[]{:S(2)}) copy-start(bf16[985,512]{1,0:T(8,128)(2,1)} %copy-done.26) | copy-start | bytes 3025924
  780.5 27.0 %copy-start.100 = (bf16[1,512,8]{1,0,2:T(2,128)(2,1)S(1)}, bf16[1,512,8]{1,0,2:T(2,128)(2,1)}, u32[]{:S(2)}) copy-start(bf16[1,512,8]{1,0,2:T(2,128)(2,1)} %get-tuple-element.122) | copy-start | bytes 24580
  795.1 254.2 %reduce-scatter.12.cloned.1.call-start = ((), (), s32[]{:S(2)}) async-start(), calls=%async_computation.17 | async-start | bytes 6389760 | tf_op jit(solution)/shard_map/reduce_scatter | solution.py:44
  861.6 18.9 %copy-start.19 = (s32[1,985,2]{2,1,0:T(8,128)S(1)}, s32[1,985,2]{2,1,0:T(8,128)}, u32[]{:S(2)}) copy-start(s32[1,985,2]{2,1,0:T(8,128)} %copy-done.17) | copy-start | bytes 23644
  882.9 9.0 copy-start.116
  891.8 8.2 copy-start.150
  960.0 105.3 %copy-start.104 = (s32[985]{0:T(1024)S(1)}, s32[985]{0:T(1024)}, u32[]{:S(2)}) copy-start(s32[985]{0:T(1024)} %copy-done.102) | copy-start | bytes 11824
  960.0 105.3 %copy-start.119 = (s32[985]{0:T(1024)S(1)}, s32[985]{0:T(1024)}, u32[]{:S(2)}) copy-start(s32[985]{0:T(1024)} %copy-done.117) | copy-start | bytes 11824
  960.0 105.3 %copy-start.139 = (f32[985]{0:T(1024)S(1)}, f32[985]{0:T(1024)}, u32[]{:S(2)}) copy-start(f32[985]{0:T(1024)} %copy-done.138) | copy-start | bytes 11824
  960.0 105.3 %copy-start.141 = (f32[985]{0:T(1024)S(1)}, f32[985]{0:T(1024)}, u32[]{:S(2)}) copy-start(f32[985]{0:T(1024)} %copy-done.140) | copy-start | bytes 11824
  960.1 105.3 %copy-start.142 = (f32[985]{0:T(1024)S(1)}, f32[985]{0:T(1024)}, u32[]{:S(2)}) copy-start(f32[985]{0:T(1024)} %get-tuple-element.97) | copy-start | bytes 11824
  960.1 157.8 %all-gather.21.cloned.1.call-start = ((), (), s32[]{:S(2)}) async-start(), calls=%async_computation.18 | async-start | bytes 3194880 | tf_op jit(solution)/shard_map/all_gather | solution.py:48
  1065.3 220.4 %all-gather.29.cloned.1.call-start = ((), (), s32[]{:S(2)}) async-start(), calls=%async_computation.23 | async-start | bytes 10158080 | tf_op jit(solution)/shard_map/all_gather | solution.py:8
  1065.4 55.2 %copy-start.161 = (s32[985]{0:T(1024)S(1)}, s32[985]{0:T(1024)}, u32[]{:S(2)}) copy-start(s32[985]{0:T(1024)} %get-tuple-element.72) | copy-start | bytes 11824
  1065.4 55.2 %copy-start.163 = (s32[985]{0:T(1024)S(1)}, s32[985]{0:T(1024)}, u32[]{:S(2)}) copy-start(s32[985]{0:T(1024)} %get-tuple-element.73) | copy-start | bytes 11824
  1142.0 322.3 %reduce-scatter.14.cloned.1.call-start = ((), (), s32[]{:S(2)}) async-start(), calls=%async_computation.19 | async-start | bytes 6389760 | tf_op jit(solution)/shard_map/reduce_scatter | solution.py:44
  1153.3 138.2 %copy-start.10 = (f32[985,512]{1,0:T(8,128)S(1)}, f32[985,512]{1,0:T(8,128)}, u32[]{:S(2)}) copy-start(f32[985,512]{1,0:T(8,128)} %copy-done.9) | copy-start | bytes 6051844
  1153.3 138.2 %copy-start.95 = (f32[985]{0:T(1024)S(1)}, f32[985]{0:T(1024)}, u32[]{:S(2)}) copy-start(f32[985]{0:T(1024)} %copy-done.94) | copy-start | bytes 11824
  1153.3 138.2 %copy-start.115 = (f32[985]{0:T(1024)S(1)}, f32[985]{0:T(1024)}, u32[]{:S(2)}) copy-start(f32[985]{0:T(1024)} %copy-done.114) | copy-start | bytes 11824
  1153.3 138.2 %copy-start.133 = (f32[512]{0:T(512)S(1)}, f32[512]{0:T(512)}, u32[]{:S(2)}) copy-start(f32[512]{0:T(512)} %get-tuple-element.83) | copy-start | bytes 6148
  1376.1 104.5 %copy-start.60 = (bf16[985,128]{0,1:T(8,128)(2,1)S(1)}, bf16[985,128]{0,1:T(8,128)(2,1)}, u32[]{:S(2)}) copy-start(bf16[985,128]{0,1:T(8,128)(2,1)} %copy-done.59) | copy-start | bytes 756484
  1376.1 156.9 %all-gather.23.cloned.1.call-start = ((), (), s32[]{:S(2)}) async-start(), calls=%async_computation.20 | async-start | bytes 3194880 | tf_op jit(solution)/shard_map/all_gather | solution.py:48
  1465.7 17.5 copy-start.11
  1480.4 144.1 %all-reduce.6.cloned.1.call-start = ((), (), s32[]{:S(2)}) async-start(), calls=%async_computation.26 | async-start | bytes 4194304
  1485.1 50.6 %copy-start.156 = (s32[985]{0:T(1024)S(1)}, s32[985]{0:T(1024)}, u32[]{:S(2)}) copy-start(s32[985]{0:T(1024)} %copy-done.154) | copy-start | bytes 11824
  1485.1 50.6 %copy-start.159 = (s32[985]{0:T(1024)S(1)}, s32[985]{0:T(1024)}, u32[]{:S(2)}) copy-start(s32[985]{0:T(1024)} %copy-done.157) | copy-start | bytes 11824
  1553.1 5.2 copy-start.5
  1553.1 5.2 copy-start.93
  1553.1 5.2 copy-start.113
  1564.2 206.3 %all-gather.31.cloned.1.call-start = ((), (), s32[]{:S(2)}) async-start(), calls=%async_computation.24 | async-start | bytes 10158080 | tf_op jit(solution)/shard_map/all_gather | solution.py:8
  1567.7 246.5 %reduce-scatter.16.cloned.1.call-start = ((), (), s32[]{:S(2)}) async-start(), calls=%async_computation.25 | async-start | bytes 294912
  1601.7 5.7 copy-start.54
  (116 other events, 254.6 us)
Sparse Core Ops, SparseCore 0:
  61.6 145.6 all-gather.24
  293.3 88.0 reduce-scatter.7
  397.5 52.4 all-gather.16
  476.5 143.4 all-gather.26
  691.0 88.0 reduce-scatter.9
  795.3 52.4 all-gather.18
  960.1 89.1 reduce-scatter.11
  1065.4 52.4 all-gather.20
  1142.1 143.4 all-gather.28
  1376.3 88.0 reduce-scatter.13
  1480.5 52.4 all-gather.22
  1564.3 60.1 all-reduce.5
  1626.1 144.3 all-gather.30
  1782.3 31.8 reduce-scatter.15
